TPU v7x, 32 devices: a whole 2x2x4 slice. The times are simulated.
32 devices in a mesh: sens: 2 (over x), sx: 4 (over z), sy: 4 (over y, core).
Axes of the slice: x: 2, y: 2, z: 4, core: 2. Of those that a mesh axis runs over, the one named last changes fastest.
Arguments:
- records: bfloat16 [4, 128, 128], P(None, 'sens'), may hold values from -6 to 6
- kernel: bfloat16 [128, 64, 32, 128], P('sens', 'sx', 'sy'), may hold values from -0.09375 to 0.09375
- diffusion: float32 [64, 32], P('sx', 'sy'), may hold values from 0.04 to 0.24
Outputs:
- predicted: float32 [4, 128, 128], P(None, ('sens', 'sx', 'sy'))
All inputs are finite; a program needn't handle non-finite values.
Results may differ from a plain program's by a relative error of at most 0.0011.
Values may be sent and summed in bfloat16 or wider, within the bound.
A program may use at most 64 MiB of HBM per device.

v0:
```python
import jax
import jax.numpy as jnp
from jax import lax
from jax.sharding import PartitionSpec as P

SWEEPS = 4


def extended(shard, sides, width):
    for axis, dim in sides:
        count, length = (lax.axis_size(axis), shard.shape[dim])
        up = [(i, (i + 1) % count) for i in range(count - 1)]
        down = [(j, i) for i, j in up]
        last = lax.slice_in_dim(shard, length - width, length, axis=dim)
        first = lax.slice_in_dim(shard, 0, width, axis=dim)
        before = lax.ppermute(last, axis, up)
        after = lax.ppermute(first, axis, down)
        shard = jnp.concatenate([before, shard, after], axis=dim)
    return shard


def neighbours(padded):
    return padded[:, 2:, 1:-1] + padded[:, :-2, 1:-1] + padded[:, 1:-1, 2:] + padded[:, 1:-1, :-2]


def smooth(prior_field, diffusion):
    weights = diffusion[None, :, :, None]
    margin = SWEEPS
    padded, rate_wide = (
        extended(prior_field, (("sx", 1), ("sy", 2)), margin),
        extended(weights, (("sx", 1), ("sy", 2)), margin),
    )
    for repeat in range(margin):
        interior = padded[:, 1:-1, 1:-1]
        rate_wide = rate_wide[:, 1:-1, 1:-1]
        padded = interior + rate_wide * (neighbours(padded) - 4.0 * interior)
    return padded


def per_device(records, kernel, diffusion):
    vectors, sensors, window = records.shape
    cells_x, cells_y = diffusion.shape
    kernel_rows = kernel.reshape(kernel.shape[0], cells_x * cells_y, window)
    partials = lax.conv_general_dilated(
        records,
        kernel_rows,
        (1,),
        [(0, window - 1)],
        dimension_numbers=("NCH", "IOH", "NCH"),
        preferred_element_type=jnp.float32,
    )
    partials = partials.reshape(vectors, cells_x, cells_y, window)
    whole_sum = lax.psum(partials, "sens")
    smoothed = smooth(whole_sum, diffusion).astype(jnp.bfloat16)
    flipped = smoothed.reshape(vectors, cells_x * cells_y, window)[:, :, ::-1]
    backward = lax.conv_general_dilated(
        flipped,
        kernel_rows,
        (1,),
        [(0, window - 1)],
        dimension_numbers=("NCH", "OIH", "NCH"),
        preferred_element_type=jnp.float32,
    )
    summands = backward[:, :, ::-1]
    return lax.psum_scatter(summands, ("sx", "sy"), scatter_dimension=1, tiled=True)


def solution(mesh):
    return jax.shard_map(
        per_device,
        mesh=mesh,
        in_specs=(P(None, "sens", None), P("sens", "sx", "sy", None), P("sx", "sy")),
        out_specs=P(None, ("sens", "sx", "sy"), None),
        check_vma=False,
    )
```

profile of v0, /device:TPU:8, one launch (start us, length us, event | category | flops | bytes accessed | tf_op | source)
XLA Modules:
  0.0 175.8 jit_solution(15188670381473331746)
XLA Ops:
  6.5 0.8 fusion.17
  7.4 1.9 %collective-permute-start.5 = (f32[1,4,8,1]{1,2,3,0:T(8,128)S(1)}, f32[1,4,8,1]{1,2,3,0:T(8,128)S(1)}, u32[]{:S(2)}, u32[]{:S(2)}) collective-permute-start(f32[1,4,8,1]{1,2,3,0:T(8,128)S(1)} %get-tuple-element.12), channel_id=1, source_target_pairs={{4,0},{8,4},{12,8},{5,1},{9,5},{13,9},{6,2},{10,6},{14,10},{7,3},{... | collective-permute-start | bytes 392 | tf_op jit(solution)/shard_map/ppermute | solution.py:17
  9.3 3.9 %collective-permute-start.4 = (f32[1,4,8,1]{1,2,3,0:T(8,128)S(1)}, f32[1,4,8,1]{1,2,3,0:T(8,128)S(1)}, u32[]{:S(2)}, u32[]{:S(2)}) collective-permute-start(f32[1,4,8,1]{1,2,3,0:T(8,128)S(1)} %get-tuple-element.11), channel_id=1, source_target_pairs={{0,4},{4,8},{8,12},{1,5},{5,9},{9,13},{2,6},{6,10},{10,14},{3,7},{... | collective-permute-start | bytes 392 | tf_op jit(solution)/shard_map/ppermute | solution.py:16
  13.2 1.0 copy.22
  14.2 3.3 %copy.23 = bf16[64,128,128]{1,0,2:T(8,128)(2,1)S(1)} copy(bf16[64,128,128]{2,1,0:T(8,128)(2,1)} %bitcast.16) | data formatting | bytes 4194304 | tf_op jit(solution)/shard_map/reshape | solution.py:43
  17.6 1.3 collective-permute-start.7
  18.9 3.0 %collective-permute-start.6 = (f32[1,24,4,1]{1,2,3,0:T(4,128)S(1)}, f32[1,24,4,1]{1,2,3,0:T(4,128)S(1)}, u32[]{:S(2)}, u32[]{:S(2)}) collective-permute-start(f32[1,24,4,1]{1,2,3,0:T(4,128)S(1)} %get-tuple-element.9), channel_id=1, source_target_pairs={{0,1},{1,2},{2,3},{4,5},{5,6},{6,7},{8,9},{9,10},{10,11},{12,13},{... | collective-permute-start | bytes 1160 | tf_op jit(solution)/shard_map/ppermute | solution.py:16
  22.0 2.9 %fusion.18 = f32[4,128,128]{1,0,2:T(4,128)S(1)} fusion(bf16[4,64,128]{1,0,2:T(4,128)(2,1)S(1)} %copy.22, bf16[64,128,128]{1,0,2:T(8,128)(2,1)S(1)} %copy.23), kind=kOutput, calls=%fused_computation.40 | convolution fusion | flops 541065216 | bytes 2424832 | tf_op jit(solution)/shard_map/conv_general_dilated | solution.py:44
  24.9 0.8 copy.24
  26.1 23.3 %all-reduce.4.cloned.1.call-done = f32[4,16,8,128]{3,2,1,0:T(8,128)} async-done(((f32[4,16,8,128]{3,2,1,0:T(8,128)}), f32[4,16,8,128]{3,2,1,0:T(8,128)}) %all-reduce.4.cloned.1.call-update) | async-done | bytes 262160 | tf_op jit(solution)/shard_map/psum | solution.py:53
  49.4 0.9 fusion.15
  50.3 3.4 %collective-permute-start = (f32[4,4,8,128]{3,2,1,0:T(8,128)S(1)}, f32[4,4,8,128]{3,2,1,0:T(8,128)S(1)}, u32[]{:S(2)}, u32[]{:S(2)}) collective-permute-start(f32[4,4,8,128]{3,2,1,0:T(8,128)S(1)} %get-tuple-element.8), channel_id=1, source_target_pairs={{0,4},{4,8},{8,12},{1,5},{5,9},{9,13},{2,6},{6,10},{10,14},{3,7},{... | collective-permute-start | bytes 196616 | tf_op jit(solution)/shard_map/ppermute | solution.py:16
  53.9 2.4 %collective-permute-start.1 = (f32[4,4,8,128]{3,2,1,0:T(8,128)S(1)}, f32[4,4,8,128]{3,2,1,0:T(8,128)S(1)}, u32[]{:S(2)}, u32[]{:S(2)}) collective-permute-start(f32[4,4,8,128]{3,2,1,0:T(8,128)S(1)} %get-tuple-element.7), channel_id=1, source_target_pairs={{4,0},{8,4},{12,8},{5,1},{9,5},{13,9},{6,2},{10,6},{14,10},{7,3},{... | collective-permute-start | bytes 196616 | tf_op jit(solution)/shard_map/ppermute | solution.py:17
  56.4 1.0 constant_dynamic-update-slice_fusion.1
  57.4 2.7 %collective-permute-done.1 = f32[4,4,8,128]{3,2,1,0:T(8,128)S(1)} collective-permute-done((f32[4,4,8,128]{3,2,1,0:T(8,128)S(1)}, f32[4,4,8,128]{3,2,1,0:T(8,128)S(1)}, u32[]{:S(2)}, u32[]{:S(2)}) %collective-permute-start.1) | collective-permute-done | bytes 65568 | tf_op jit(solution)/shard_map/ppermute | solution.py:17
  60.1 1.3 collective-permute-start.3
  61.4 3.0 %collective-permute-start.2 = (f32[4,24,4,128]{3,2,1,0:T(4,128)S(1)}, f32[4,24,4,128]{3,2,1,0:T(4,128)S(1)}, u32[]{:S(2)}, u32[]{:S(2)}) collective-permute-start(f32[4,24,4,128]{3,2,1,0:T(4,128)S(1)} %get-tuple-element.5), channel_id=1, source_target_pairs={{0,1},{1,2},{2,3},{4,5},{5,6},{6,7},{8,9},{9,10},{10,11},{12,13},{... | collective-permute-start | bytes 589832 | tf_op jit(solution)/shard_map/ppermute | solution.py:16
  64.7 0.9 collective-permute-done.2
  67.2 6.1 %fusion.19 = f32[4,64,128]{1,0,2:T(4,128)S(1)} fusion(bf16[4,128,128]{1,0,2:T(4,128)(2,1)S(1)} %copy.29, bf16[64,128,128]{1,0,2:T(8,128)(2,1)S(1)} %copy.23), kind=kOutput, calls=%fused_computation.41 | convolution fusion | flops 541065216 | bytes 2359296 | tf_op jit(solution)/shard_map/conv_general_dilated | solution.py:56
  73.3 0.8 copy.31
  74.2 0.6 dynamic-slice
  75.4 92.2 %all-reduce.6.cloned.1.call-done = f32[4,64,128]{2,0,1:T(4,128)} async-done(((f32[4,64,128]{2,0,1:T(4,128)}), f32[4,64,128]{2,0,1:T(4,128)}) %all-reduce.6.cloned.1.call-update) | async-done | bytes 131088
  167.6 0.7 constant_dynamic-slice_fusion
  168.3 0.6 copy.32
  (35 shorter events, 2.6 us)
Async XLA Ops:
  6.5 42.8 %all-reduce.4.cloned.1.call-start = ((), (), s32[]{:S(2)}) async-start(), calls=%async_computation | async-start | bytes 524288 | tf_op jit(solution)/shard_map/psum | solution.py:53
  7.4 10.1 %collective-permute-start.5 = (f32[1,4,8,1]{1,2,3,0:T(8,128)S(1)}, f32[1,4,8,1]{1,2,3,0:T(8,128)S(1)}, u32[]{:S(2)}, u32[]{:S(2)}) collective-permute-start(f32[1,4,8,1]{1,2,3,0:T(8,128)S(1)} %get-tuple-element.12), channel_id=1, source_target_pairs={{4,0},{8,4},{12,8},{5,1},{9,5},{13,9},{6,2},{10,6},{14,10},{7,3},{... | collective-permute-start | bytes 392 | tf_op jit(solution)/shard_map/ppermute | solution.py:17
  9.3 8.2 %collective-permute-start.4 = (f32[1,4,8,1]{1,2,3,0:T(8,128)S(1)}, f32[1,4,8,1]{1,2,3,0:T(8,128)S(1)}, u32[]{:S(2)}, u32[]{:S(2)}) collective-permute-start(f32[1,4,8,1]{1,2,3,0:T(8,128)S(1)} %get-tuple-element.11), channel_id=1, source_target_pairs={{0,4},{4,8},{8,12},{1,5},{5,9},{9,13},{2,6},{6,10},{10,14},{3,7},{... | collective-permute-start | bytes 392 | tf_op jit(solution)/shard_map/ppermute | solution.py:16
  14.2 3.3 %copy-start = (f32[16,8]{0,1:T(8,128)S(1)}, f32[16,8]{0,1:T(8,128)}, u32[]{:S(2)}) copy-start(f32[16,8]{0,1:T(8,128)} %param.5) | copy-start | bytes 1540
  17.6 8.3 %collective-permute-start.7 = (f32[1,24,4,1]{1,2,3,0:T(4,128)S(1)}, f32[1,24,4,1]{1,2,3,0:T(4,128)S(1)}, u32[]{:S(2)}, u32[]{:S(2)}) collective-permute-start(f32[1,24,4,1]{1,2,3,0:T(4,128)S(1)} %get-tuple-element.10), channel_id=1, source_target_pairs={{1,0},{2,1},{3,2},{5,4},{6,5},{7,6},{9,8},{10,9},{11,10},{13,12},{... | collective-permute-start | bytes 1160 | tf_op jit(solution)/shard_map/ppermute | solution.py:17
  18.9 7.0 %collective-permute-start.6 = (f32[1,24,4,1]{1,2,3,0:T(4,128)S(1)}, f32[1,24,4,1]{1,2,3,0:T(4,128)S(1)}, u32[]{:S(2)}, u32[]{:S(2)}) collective-permute-start(f32[1,24,4,1]{1,2,3,0:T(4,128)S(1)} %get-tuple-element.9), channel_id=1, source_target_pairs={{0,1},{1,2},{2,3},{4,5},{5,6},{6,7},{8,9},{9,10},{10,11},{12,13},{... | collective-permute-start | bytes 1160 | tf_op jit(solution)/shard_map/ppermute | solution.py:16
  25.8 141.9 %all-reduce.6.cloned.1.call-start = ((), (), s32[]{:S(2)}) async-start(), calls=%async_computation.1 | async-start | bytes 262144
  50.3 6.2 %collective-permute-start = (f32[4,4,8,128]{3,2,1,0:T(8,128)S(1)}, f32[4,4,8,128]{3,2,1,0:T(8,128)S(1)}, u32[]{:S(2)}, u32[]{:S(2)}) collective-permute-start(f32[4,4,8,128]{3,2,1,0:T(8,128)S(1)} %get-tuple-element.8), channel_id=1, source_target_pairs={{0,4},{4,8},{8,12},{1,5},{5,9},{9,13},{2,6},{6,10},{10,14},{3,7},{... | collective-permute-start | bytes 196616 | tf_op jit(solution)/shard_map/ppermute | solution.py:16
  53.9 6.1 %collective-permute-start.1 = (f32[4,4,8,128]{3,2,1,0:T(8,128)S(1)}, f32[4,4,8,128]{3,2,1,0:T(8,128)S(1)}, u32[]{:S(2)}, u32[]{:S(2)}) collective-permute-start(f32[4,4,8,128]{3,2,1,0:T(8,128)S(1)} %get-tuple-element.7), channel_id=1, source_target_pairs={{4,0},{8,4},{12,8},{5,1},{9,5},{13,9},{6,2},{10,6},{14,10},{7,3},{... | collective-permute-start | bytes 196616 | tf_op jit(solution)/shard_map/ppermute | solution.py:17
  60.1 4.5 %collective-permute-start.3 = (f32[4,24,4,128]{3,2,1,0:T(4,128)S(1)}, f32[4,24,4,128]{3,2,1,0:T(4,128)S(1)}, u32[]{:S(2)}, u32[]{:S(2)}) collective-permute-start(f32[4,24,4,128]{3,2,1,0:T(4,128)S(1)} %get-tuple-element.6), channel_id=1, source_target_pairs={{1,0},{2,1},{3,2},{5,4},{6,5},{7,6},{9,8},{10,9},{11,10},{13,12},{... | collective-permute-start | bytes 589832 | tf_op jit(solution)/shard_map/ppermute | solution.py:17
  61.4 4.1 %collective-permute-start.2 = (f32[4,24,4,128]{3,2,1,0:T(4,128)S(1)}, f32[4,24,4,128]{3,2,1,0:T(4,128)S(1)}, u32[]{:S(2)}, u32[]{:S(2)}) collective-permute-start(f32[4,24,4,128]{3,2,1,0:T(4,128)S(1)} %get-tuple-element.5), channel_id=1, source_target_pairs={{0,1},{1,2},{2,3},{4,5},{5,6},{6,7},{8,9},{9,10},{10,11},{12,13},{... | collective-permute-start | bytes 589832 | tf_op jit(solution)/shard_map/ppermute | solution.py:16
  66.6 7.6 %copy-start.1 = (u32[32]{0:T(128)S(1)}, u32[32]{0:T(128)}, u32[]{:S(2)}) copy-start(u32[32]{0:T(128)} %constant.3) | copy-start | bytes 388
Sparse Core Ops, SparseCore 0:
  25.9 23.4 all-reduce.3
  74.3 93.3 all-reduce.5
where the time goes:
time: 176 us
  waiting for transfers between devices  119 us (68%)
  starting transfers between devices  20.4 us (12%)
  between operations  14.3 us (8%)
  local copies, waits for them, and re-layouts  11.7 us (7%)
  matrix products  9.06 us (5%)
    unnamed x3, waiting for transfers between devices  92.3 us
    psum x1, waiting for transfers between devices, per_device(): whole_sum = lax.psum(partials, 'sens')  23.3 us
    ppermute x4, starting transfers between devices, extended(): before = lax.ppermute(last, axis, up)  13.4 us
    ppermute x4, starting transfers between devices, extended(): after = lax.ppermute(first, axis, down)  6.92 us
    conv_general_dilated x1, matrix products, per_device(): lax.conv_general_dilated(flipped, kernel_rows, (1,), [(0, window - 1)], d...  6.13 us
  transfers between devices with their start and end apart: 10, of which 4 were waited for; matrix products, arithmetic and copies ran while one was open for 6% of the time, Pallas kernels for 0%

commit v1 on v0

--- a/solution.py
+++ b/solution.py
@@ -50,7 +50,7 @@
         preferred_element_type=jnp.float32,
     )
     partials = partials.reshape(vectors, cells_x, cells_y, window)
-    whole_sum = lax.psum(partials, "sens")
+    whole_sum = lax.all_gather(partials, "sens").sum(axis=0)
     smoothed = smooth(whole_sum, diffusion).astype(jnp.bfloat16)
     flipped = smoothed.reshape(vectors, cells_x * cells_y, window)[:, :, ::-1]
     backward = lax.conv_general_dilated(

time: 176 us -> 161 us (0.915)
  waiting for transfers between devices: 119 us -> 100 us
  blocking collectives: 0 us -> 8.15 us
  local copies, waits for them, and re-layouts: 11.7 us -> 8.35 us
    psum x1 -> x0, waiting for transfers between devices: 23.3 us -> none  [per_device(): whole_sum = lax.psum(partials, 'sens')]
    all_gather x0 -> x1, blocking collectives: none -> 8.15 us  [per_device(): whole_sum = lax.all_gather(partials, 'sens').sum(axis=0)]
    ppermute x4, waiting for transfers between devices: 2.68 us -> 7.82 us  [extended(): after = lax.ppermute(first, axis, down)]
    unnamed x10, local copies, waits for them, and re-layouts: 3.31 us -> 1.51 us
    ppermute x4, starting transfers between devices: 13.4 us -> 11.6 us  [extended(): before = lax.ppermute(last, axis, up)]
    unnamed x3 -> x2, waiting for transfers between devices: 92.3 us -> 92.7 us
  transfers between devices with their start and end apart: 10 -> 9, of which waited for: 4 -> 3; matrix products, arithmetic and copies ran while one was open for 6% -> 5% of each run, Pallas kernels for 0% -> 0%
where the time goes in v1:
time: 161 us; the launch traced here: 160 us
  waiting for transfers between devices  100 us (62%)
  starting transfers between devices  18.9 us (12%)
  between operations  14.3 us (9%)
  matrix products  9.06 us (6%)
  local copies, waits for them, and re-layouts  8.35 us (5%)
  blocking collectives  8.15 us (5%)
    unnamed x2, waiting for transfers between devices  92.7 us
    ppermute x4, starting transfers between devices, extended(): before = lax.ppermute(last, axis, up)  11.6 us
    all_gather x1, blocking collectives, per_device(): whole_sum = lax.all_gather(partials, 'sens').sum(axis=0)  8.15 us
    ppermute x4, waiting for transfers between devices, extended(): after = lax.ppermute(first, axis, down)  7.82 us
    ppermute x4, starting transfers between devices, extended(): after = lax.ppermute(first, axis, down)  7.29 us
    conv_general_dilated x1, matrix products, per_device(): lax.conv_general_dilated(flipped, kernel_rows, (1,), [(0, window - 1)], d...  6.13 us
    reshape x1, local copies, waits for them, and re-layouts, per_device(): kernel_rows = kernel.reshape(kernel.shape[0], cells_x * cells_y, window)  3.33 us
  transfers between devices with their start and end apart: 9, of which 3 were waited for; matrix products, arithmetic and copies ran while one was open for 5% of the time, Pallas kernels for 0%

profile of v1, /device:TPU:8, one launch (start us, length us, event | category | flops | bytes accessed | tf_op | source)
XLA Modules:
  0.0 160.5 jit_solution(4046373324256067279)
XLA Ops:
  6.5 0.8 fusion.17
  7.4 3.5 %collective-permute-start.4 = (f32[1,4,8,1]{1,2,3,0:T(8,128)S(1)}, f32[1,4,8,1]{1,2,3,0:T(8,128)S(1)}, u32[]{:S(2)}, u32[]{:S(2)}) collective-permute-start(f32[1,4,8,1]{1,2,3,0:T(8,128)S(1)} %get-tuple-element.11), channel_id=1, source_target_pairs={{0,4},{4,8},{8,12},{1,5},{5,9},{9,13},{2,6},{6,10},{10,14},{3,7},{... | collective-permute-start | bytes 392 | tf_op jit(solution)/shard_map/ppermute | solution.py:16
  10.9 2.4 %collective-permute-start.5 = (f32[1,4,8,1]{1,2,3,0:T(8,128)S(1)}, f32[1,4,8,1]{1,2,3,0:T(8,128)S(1)}, u32[]{:S(2)}, u32[]{:S(2)}) collective-permute-start(f32[1,4,8,1]{1,2,3,0:T(8,128)S(1)} %get-tuple-element.12), channel_id=1, source_target_pairs={{4,0},{8,4},{12,8},{5,1},{9,5},{13,9},{6,2},{10,6},{14,10},{7,3},{... | collective-permute-start | bytes 392 | tf_op jit(solution)/shard_map/ppermute | solution.py:17
  13.2 3.3 %copy.23 = bf16[64,128,128]{1,0,2:T(8,128)(2,1)S(1)} copy(bf16[64,128,128]{2,1,0:T(8,128)(2,1)} %bitcast.16) | data formatting | bytes 4194304 | tf_op jit(solution)/shard_map/reshape | solution.py:43
  16.7 2.9 %fusion.18 = f32[4,128,128]{1,0,2:T(4,128)S(1)} fusion(bf16[4,64,128]{1,0,2:T(4,128)(2,1)S(1)} %copy.22, bf16[64,128,128]{1,0,2:T(8,128)(2,1)S(1)} %copy.23), kind=kOutput, calls=%fused_computation.38 | convolution fusion | flops 541065216 | bytes 2424832 | tf_op jit(solution)/shard_map/conv_general_dilated | solution.py:44
  19.8 8.2 %all_gather.3 = f32[2,4,16,8,128]{4,3,2,1,0:T(8,128)S(1)} all-gather(f32[1,4,16,8,128]{4,3,2,1,0:T(8,128)S(1)} %bitcast.17), channel_id=1, replica_groups=mesh['sens'=2,'sx'=4,'sy'=4] {'sens'}, dimensions={0}, use_global_device_ids=true | all-gather | bytes 786432 | tf_op jit(solution)/shard_map/all_gather | solution.py:53
  28.1 1.3 collective-permute-start.6
  29.4 1.3 collective-permute-start.7
  30.7 3.5 %collective-permute-start = (f32[4,4,8,128]{3,2,1,0:T(8,128)S(1)}, f32[4,4,8,128]{3,2,1,0:T(8,128)S(1)}, u32[]{:S(2)}, u32[]{:S(2)}) collective-permute-start(f32[4,4,8,128]{3,2,1,0:T(8,128)S(1)} %get-tuple-element.7), channel_id=1, source_target_pairs={{0,4},{4,8},{8,12},{1,5},{5,9},{9,13},{2,6},{6,10},{10,14},{3,7},{... | collective-permute-start | bytes 196616 | tf_op jit(solution)/shard_map/ppermute | solution.py:16
  34.2 2.4 %collective-permute-start.1 = (f32[4,4,8,128]{3,2,1,0:T(8,128)S(1)}, f32[4,4,8,128]{3,2,1,0:T(8,128)S(1)}, u32[]{:S(2)}, u32[]{:S(2)}) collective-permute-start(f32[4,4,8,128]{3,2,1,0:T(8,128)S(1)} %get-tuple-element.8), channel_id=1, source_target_pairs={{4,0},{8,4},{12,8},{5,1},{9,5},{13,9},{6,2},{10,6},{14,10},{7,3},{... | collective-permute-start | bytes 196616 | tf_op jit(solution)/shard_map/ppermute | solution.py:17
  37.1 3.3 %collective-permute-done.1 = f32[4,4,8,128]{3,2,1,0:T(8,128)S(1)} collective-permute-done((f32[4,4,8,128]{3,2,1,0:T(8,128)S(1)}, f32[4,4,8,128]{3,2,1,0:T(8,128)S(1)}, u32[]{:S(2)}, u32[]{:S(2)}) %collective-permute-start.1) | collective-permute-done | bytes 65568 | tf_op jit(solution)/shard_map/ppermute | solution.py:17
  40.5 3.4 %collective-permute-start.2 = (f32[4,24,4,128]{3,2,1,0:T(4,128)S(1)}, f32[4,24,4,128]{3,2,1,0:T(4,128)S(1)}, u32[]{:S(2)}, u32[]{:S(2)}) collective-permute-start(f32[4,24,4,128]{3,2,1,0:T(4,128)S(1)} %get-tuple-element.5), channel_id=1, source_target_pairs={{0,1},{1,2},{2,3},{4,5},{5,6},{6,7},{8,9},{9,10},{10,11},{12,13},{... | collective-permute-start | bytes 589832 | tf_op jit(solution)/shard_map/ppermute | solution.py:16
  43.8 1.3 collective-permute-start.3
  45.3 4.5 %collective-permute-done.3 = f32[4,24,4,128]{3,2,1,0:T(4,128)S(1)} collective-permute-done((f32[4,24,4,128]{3,2,1,0:T(4,128)S(1)}, f32[4,24,4,128]{3,2,1,0:T(4,128)S(1)}, u32[]{:S(2)}, u32[]{:S(2)}) %collective-permute-start.3) | collective-permute-done | bytes 196640 | tf_op jit(solution)/shard_map/ppermute | solution.py:17
  50.0 0.3 fusion.2
  50.3 0.3 fusion.5
  50.5 0.2 fusion.8
  50.9 0.4 rev.6
  51.5 6.1 %fusion.19 = f32[4,64,128]{1,0,2:T(4,128)S(1)} fusion(bf16[4,128,128]{1,0,2:T(4,128)(2,1)S(1)} %copy.29, bf16[64,128,128]{1,0,2:T(8,128)(2,1)S(1)} %copy.23), kind=kOutput, calls=%fused_computation.39 | convolution fusion | flops 541065216 | bytes 2359296 | tf_op jit(solution)/shard_map/conv_general_dilated | solution.py:56
  57.6 0.8 copy.31
  58.5 0.6 dynamic-slice
  59.7 92.6 %all-reduce.3.cloned.1.call-done = f32[4,64,128]{2,0,1:T(4,128)} async-done(((f32[4,64,128]{2,0,1:T(4,128)}), f32[4,64,128]{2,0,1:T(4,128)}) %all-reduce.3.cloned.1.call-update) | async-done | bytes 131088
  152.3 0.7 constant_dynamic-slice_fusion
  153.0 0.6 copy.32
  (34 shorter events, 1.6 us)
Async XLA Ops:
  6.5 145.8 %all-reduce.3.cloned.1.call-start = ((), (), s32[]{:S(2)}) async-start(), calls=%async_computation | async-start | bytes 262144
  7.4 20.6 %collective-permute-start.4 = (f32[1,4,8,1]{1,2,3,0:T(8,128)S(1)}, f32[1,4,8,1]{1,2,3,0:T(8,128)S(1)}, u32[]{:S(2)}, u32[]{:S(2)}) collective-permute-start(f32[1,4,8,1]{1,2,3,0:T(8,128)S(1)} %get-tuple-element.11), channel_id=1, source_target_pairs={{0,4},{4,8},{8,12},{1,5},{5,9},{9,13},{2,6},{6,10},{10,14},{3,7},{... | collective-permute-start | bytes 392 | tf_op jit(solution)/shard_map/ppermute | solution.py:16
  10.9 17.2 %collective-permute-start.5 = (f32[1,4,8,1]{1,2,3,0:T(8,128)S(1)}, f32[1,4,8,1]{1,2,3,0:T(8,128)S(1)}, u32[]{:S(2)}, u32[]{:S(2)}) collective-permute-start(f32[1,4,8,1]{1,2,3,0:T(8,128)S(1)} %get-tuple-element.12), channel_id=1, source_target_pairs={{4,0},{8,4},{12,8},{5,1},{9,5},{13,9},{6,2},{10,6},{14,10},{7,3},{... | collective-permute-start | bytes 392 | tf_op jit(solution)/shard_map/ppermute | solution.py:17
  13.2 3.4 %copy-start.1 = (bf16[4,64,128]{2,1,0:T(8,128)(2,1)S(1)}, bf16[4,64,128]{2,1,0:T(8,128)(2,1)}, u32[]{:S(2)}) copy-start(bf16[4,64,128]{2,1,0:T(8,128)(2,1)} %param.3) | copy-start | bytes 196612
  16.7 11.3 %copy-start = (f32[16,8]{0,1:T(8,128)S(1)}, f32[16,8]{0,1:T(8,128)}, u32[]{:S(2)}) copy-start(f32[16,8]{0,1:T(8,128)} %param.5) | copy-start | bytes 1540
  28.1 8.5 %collective-permute-start.6 = (f32[1,24,4,1]{1,2,3,0:T(4,128)S(1)}, f32[1,24,4,1]{1,2,3,0:T(4,128)S(1)}, u32[]{:S(2)}, u32[]{:S(2)}) collective-permute-start(f32[1,24,4,1]{1,2,3,0:T(4,128)S(1)} %get-tuple-element.9), channel_id=1, source_target_pairs={{0,1},{1,2},{2,3},{4,5},{5,6},{6,7},{8,9},{9,10},{10,11},{12,13},{... | collective-permute-start | bytes 1160 | tf_op jit(solution)/shard_map/ppermute | solution.py:16
  29.4 7.3 %collective-permute-start.7 = (f32[1,24,4,1]{1,2,3,0:T(4,128)S(1)}, f32[1,24,4,1]{1,2,3,0:T(4,128)S(1)}, u32[]{:S(2)}, u32[]{:S(2)}) collective-permute-start(f32[1,24,4,1]{1,2,3,0:T(4,128)S(1)} %get-tuple-element.10), channel_id=1, source_target_pairs={{1,0},{2,1},{3,2},{5,4},{6,5},{7,6},{9,8},{10,9},{11,10},{13,12},{... | collective-permute-start | bytes 1160 | tf_op jit(solution)/shard_map/ppermute | solution.py:17
  30.7 6.4 %collective-permute-start = (f32[4,4,8,128]{3,2,1,0:T(8,128)S(1)}, f32[4,4,8,128]{3,2,1,0:T(8,128)S(1)}, u32[]{:S(2)}, u32[]{:S(2)}) collective-permute-start(f32[4,4,8,128]{3,2,1,0:T(8,128)S(1)} %get-tuple-element.7), channel_id=1, source_target_pairs={{0,4},{4,8},{8,12},{1,5},{5,9},{9,13},{2,6},{6,10},{10,14},{3,7},{... | collective-permute-start | bytes 196616 | tf_op jit(solution)/shard_map/ppermute | solution.py:16
  34.2 6.2 %collective-permute-start.1 = (f32[4,4,8,128]{3,2,1,0:T(8,128)S(1)}, f32[4,4,8,128]{3,2,1,0:T(8,128)S(1)}, u32[]{:S(2)}, u32[]{:S(2)}) collective-permute-start(f32[4,4,8,128]{3,2,1,0:T(8,128)S(1)} %get-tuple-element.8), channel_id=1, source_target_pairs={{4,0},{8,4},{12,8},{5,1},{9,5},{13,9},{6,2},{10,6},{14,10},{7,3},{... | collective-permute-start | bytes 196616 | tf_op jit(solution)/shard_map/ppermute | solution.py:17
  40.5 4.8 %collective-permute-start.2 = (f32[4,24,4,128]{3,2,1,0:T(4,128)S(1)}, f32[4,24,4,128]{3,2,1,0:T(4,128)S(1)}, u32[]{:S(2)}, u32[]{:S(2)}) collective-permute-start(f32[4,24,4,128]{3,2,1,0:T(4,128)S(1)} %get-tuple-element.5), channel_id=1, source_target_pairs={{0,1},{1,2},{2,3},{4,5},{5,6},{6,7},{8,9},{9,10},{10,11},{12,13},{... | collective-permute-start | bytes 589832 | tf_op jit(solution)/shard_map/ppermute | solution.py:16
  43.8 6.0 %collective-permute-start.3 = (f32[4,24,4,128]{3,2,1,0:T(4,128)S(1)}, f32[4,24,4,128]{3,2,1,0:T(4,128)S(1)}, u32[]{:S(2)}, u32[]{:S(2)}) collective-permute-start(f32[4,24,4,128]{3,2,1,0:T(4,128)S(1)} %get-tuple-element.6), channel_id=1, source_target_pairs={{1,0},{2,1},{3,2},{5,4},{6,5},{7,6},{9,8},{10,9},{11,10},{13,12},{... | collective-permute-start | bytes 589832 | tf_op jit(solution)/shard_map/ppermute | solution.py:17
  50.9 7.6 %copy-start.2 = (u32[32]{0:T(128)S(1)}, u32[32]{0:T(128)}, u32[]{:S(2)}) copy-start(u32[32]{0:T(128)} %constant.4) | copy-start | bytes 388
Sparse Core Ops, SparseCore 0:
  58.6 93.7 all-reduce.2
